TPU v7x, 32 devices: a whole 2x2x4 slice. The times are simulated.
32 devices in a mesh: chan: 4 (over y, core), blk: 8 (over z, x).
Axes of the slice: x: 2, y: 2, z: 4, core: 2. Of those that a mesh axis runs over, the one named last changes fastest.
Arguments:
- comp_alms: float32 [3, 4, 8, 4096], P(None, None, 'blk', 'chan'), may hold values from -6 to 6
- legendre: bfloat16 [2, 8, 4096, 32], P(None, 'blk'), may hold values from -0.09375 to 0.09375
- inv_noise: float32 [4, 2, 32, 8192], P('chan', None, 'blk'), may hold values from 0.5 to 5
- beam_window: float32 [4, 4096], replicated, may hold values from 0.1 to 1
- mixing: float32 [4, 3], replicated, may hold values from 0.2 to 1.5
- channel_of: int32 [4], replicated, may hold values from 0 to 3, each once
- m_orders: int32 [8], replicated, may hold values from 0 to 4095, as said below
- cycle_of: int32 [32], replicated, may hold values from 0 to 31, each once
- cycle_pixels: int32 [32], replicated, may hold values from 4 to 8192, as said below
Outputs:
- normal_product: float32 [3, 4, 8, 4096], P(None, None, 'blk', 'chan')
Inputs may be any that keep to these rules, and one draw needn't show every extreme that they name: `m_orders`: the orders are distinct. `cycle_pixels`: each entry is 4 * min(h, 2048, 8192 - h) for some cycle number h of 1 to 8191; at least one entry equals 8192.
All inputs are finite; a program needn't handle non-finite values.
Results may differ from a plain program's by a relative error of at most 0.0022.
Values may be sent and summed in bfloat16 or wider, within the bound.
A program may use at most 128 MiB of HBM per device.

v0:
```python
import functools
import math

import jax
import jax.numpy as jnp
from jax import lax
from jax.experimental import pallas as pl
from jax.experimental.pallas import tpu as pltpu
from jax.sharding import PartitionSpec as P

F32 = jnp.float32
BF16 = jnp.bfloat16
LANES = 128
NT = (((1,), (1,)), ((), ()))
NN = (((1,), (0,)), ((), ()))


def iota(shape, dim):
    return lax.broadcasted_iota(jnp.int32, shape, dim)


def dot(left, right, dims):
    return lax.dot_general(left, right, dims, preferred_element_type=F32)


def exact_mod(value, modulus, inverse):
    rest = value - jnp.floor(value * inverse) * modulus
    rest = jnp.where(rest < 0, rest + modulus, rest)
    return jnp.where(rest >= modulus, rest - modulus, rest)


def kernel(
    chans, blks, alm_hbm, leg_hbm, inv_hbm, beam_hbm, mix_hbm, chan_hbm, order_hbm, cycle_hbm,
    pixel_hbm, cycle_row_hbm, out_ref, mix_s, chan_s, order_s, cycle_s, pixel_s, cycle_row, comp_v,
    leg_v, inv_v, beam_v, gain_v, slot_leg, phases, send1, recv1, send2, recv2, spare, in_sem, send_sem,
    recv_sem,
):
    comps = comp_v.shape[0]
    shard = comp_v.shape[2]
    cycles = leg_v.shape[1] // 4
    slots = inv_v.shape[0] // 2
    width = inv_v.shape[1]
    rows = 4 * chans
    total = chans * blks
    me_c = lax.axis_index("chan")
    me_b = lax.axis_index("blk")
    first = pl.multiple_of(me_c * shard, shard)

    def peer(offset):
        return lax.rem(me_c + offset // blks, chans), lax.rem(me_b + offset % blks, blks)

    def each_peer(act):
        if total <= 64:
            for offset in range(1, total):
                act(offset)
        else:
            lax.fori_loop(1, total, lambda offset, carry: (act(offset), carry)[1], 0)

    barrier = pltpu.get_barrier_semaphore()

    def greet(offset):
        pl.semaphore_signal(
            barrier, inc=1, device_id=peer(offset), device_id_type=pl.DeviceIdType.MESH
        )

    each_peer(greet)
    scalars = []

    def load(src, dst, group):
        copy = pltpu.make_async_copy(src, dst, in_sem.at[group])
        copy.start()
        return copy

    def loaded(dst, group):
        pltpu.make_async_copy(dst, dst, in_sem.at[group]).wait()

    for src, dst in (
        (mix_hbm, mix_s), (chan_hbm, chan_s), (order_hbm, order_s), (cycle_hbm, cycle_s),
        (pixel_hbm, pixel_s), (cycle_row_hbm, cycle_row),
    ):
        scalars.append(load(src, dst, 4 + len(scalars)))
    for comp in range(comps):
        for part in range(4):
            for half in range(2):
                load(alm_hbm.at[comp, part], comp_v.at[comp, pl.ds(4 * half + part, 1), :], 0)
    load(beam_hbm.at[:, pl.ds(first, shard)], beam_v, 1)
    for kind in range(2):
        for part in range(4):
            load(
                leg_hbm.at[kind, 0, :, pl.ds(first, shard)],
                leg_v.at[kind, pl.ds(part * cycles, cycles), :],
                2,
            )
    for stokes in range(2):
        load(inv_hbm.at[0, stokes], inv_v.at[pl.ds(stokes * slots, slots), :], 3)
    for copy in scalars:
        copy.wait()
    loaded(comp_v, 0)
    loaded(beam_v, 1)
    loaded(leg_v, 2)

    low_half = iota((8, 1), 0) < 4
    keep = (iota((1, shard), 1) + first >= order_s[me_b]).astype(F32)
    mix_cols = []
    alm_rows = []
    for pair in range(chans // 2):
        picked = [chan_s[2 * pair], chan_s[2 * pair + 1]]
        columns = [
            jnp.where(low_half, mix_s[picked[0], comp], mix_s[picked[1], comp])
            for comp in range(comps)
        ]
        mix_cols.append(columns)
        mixed = columns[0] * comp_v[0]
        for comp in range(1, comps):
            mixed = mixed + columns[comp] * comp_v[comp]
        beam = jnp.where(
            low_half, beam_v[pl.ds(picked[0], 1), :], beam_v[pl.ds(picked[1], 1), :]
        )
        gain = beam * keep
        gain_v[pl.ds(8 * pair, 8), :] = gain
        alm_rows.append(mixed * gain)
    alm = jnp.concatenate(alm_rows, axis=0).astype(BF16)
    plus = dot(alm, leg_v[0], NT)
    minus = dot(alm, leg_v[1], NT)
    row_part = iota(plus.shape, 0) % 4
    lane_part = iota(plus.shape, 1) // cycles
    outer = (lane_part == 0) | (lane_part == 3)
    signed = jnp.where(outer, -minus, minus)
    joined = jnp.where(lane_part == row_part, plus, 0.0) + jnp.where(
        lane_part == 3 - row_part, signed, 0.0
    )
    folded = joined
    for step in range(1, 4):
        folded = folded + pltpu.roll(joined, rows - step, 0)
    send1[...] = folded

    pl.semaphore_wait(barrier, total - 1)

    def scatter(src_of, dst, phase):
        def start(offset):
            dest_c, dest_b = peer(offset)
            pltpu.make_async_remote_copy(
                src_ref=src_of(dest_c, dest_b),
                dst_ref=dst.at[me_c, pl.ds(me_b, 1), :],
                send_sem=send_sem.at[phase],
                recv_sem=recv_sem.at[phase],
                device_id=(dest_c, dest_b),
                device_id_type=pl.DeviceIdType.MESH,
            ).start()

        each_peer(start)
        pltpu.make_async_copy(
            src_of(me_c, me_b), dst.at[me_c, pl.ds(me_b, 1), :], recv_sem.at[phase]
        ).start()
        pltpu.make_async_copy(src_of(me_c, me_b), spare.at[phase], send_sem.at[phase]).start()

    def arrived(dst, phase):
        pltpu.make_async_copy(dst, dst, recv_sem.at[phase]).wait()

    def sent(dst, phase):
        pltpu.make_async_copy(dst, dst, send_sem.at[phase]).wait()

    def by_channel(dest_c, dest_b):
        return send1.at[pl.ds(4 * dest_c, 1), :]

    def by_order(dest_c, dest_b):
        return send2.at[pl.ds(dest_b, 1), :]

    scatter(by_channel, recv1, 0)

    own_cycles = [cycle_s[me_b * slots + slot] for slot in range(slots)]
    own_pixels = [pixel_s[cycle].astype(F32) for cycle in own_cycles]

    def by_slot(slot_index, values):
        result = jnp.where(slot_index == 0, values[0], values[slots - 1])
        for slot in range(1, slots - 1):
            result = jnp.where(slot_index == slot, values[slot], result)
        return result

    grid = (slots * blks, LANES)
    row = iota(grid, 0)
    lane = iota(grid, 1).astype(F32)
    pixels = by_slot(row // blks, own_pixels)
    orders = jnp.zeros(grid, F32)
    for order in range(blks):
        orders = jnp.where(row % blks == order, order_s[order].astype(F32), orders)
    modulus = 2.0 * pixels
    inverse = 1.0 / modulus
    scale = jnp.float32(math.pi) / pixels
    fine = exact_mod(orders * (2.0 * lane + 1.0), modulus, inverse) * scale
    stride = exact_mod(orders * (2.0 * LANES), modulus, inverse)
    coarse = exact_mod(stride * lane, modulus, inverse) * scale
    fine_cos, fine_sin = jnp.cos(fine), jnp.sin(fine)
    coarse_cos, coarse_sin = jnp.cos(coarse), jnp.sin(coarse)
    half = slots * blks
    for chunk in range(width // LANES):
        turn_cos = coarse_cos[:, chunk : chunk + 1]
        turn_sin = coarse_sin[:, chunk : chunk + 1]
        window = pl.ds(chunk * LANES, LANES)
        phases[pl.ds(0, half), window] = (turn_cos * fine_cos - turn_sin * fine_sin).astype(BF16)
        phases[pl.ds(half, half), window] = (turn_sin * fine_cos + turn_cos * fine_sin).astype(
            BF16
        )

    loaded(inv_v, 3)
    row_pixels = by_slot(iota((2 * slots, 1), 0) % slots, own_pixels)
    row_inverse = 1.0 / row_pixels
    live = iota((2 * slots, width), 1).astype(F32) < row_pixels
    inv_v[...] = jnp.where(live, inv_v[...], 0.0) * row_inverse

    cycle_hot = (iota((cycles, cycles), 0) == cycle_row[...]).astype(BF16)
    to_row, to_col = iota((cycles, cycles), 0), iota((cycles, cycles), 1)
    reorder = ((to_row // blks == to_col % slots) & (to_row % blks == to_col // slots)).astype(
        F32
    ).astype(BF16)
    slot_hot = dot(reorder, cycle_hot, NT).astype(BF16)
    for kind in range(2):
        slot_leg[pl.ds(kind * cycles, cycles), :] = dot(
            slot_hot, leg_v[kind, pl.ds(0, cycles), :], NN
        ).astype(BF16)

    pick_shape = (2 * slots, 4 * cycles)
    pick_row, pick_lane = iota(pick_shape, 0), iota(pick_shape, 1)
    pick = (
        (pick_lane // (2 * cycles) == pick_row // slots)
        & (pick_lane % cycles == by_slot(pick_row % slots, own_cycles))
    ).astype(F32).astype(BF16)
    place_shape = (2 * slots, 2 * slots * rows)
    place_row, place_lane = iota(place_shape, 0), iota(place_shape, 1)
    lane_p = place_lane % 4
    lane_q = place_lane // rows
    twist = lane_q >= slots
    source_p = jnp.where(twist, 3 - lane_p, lane_p)
    fits = (
        ((place_lane // 4) % chans == me_c)
        & (lane_q % slots == place_row % slots)
        & (source_p // 2 == place_row // slots)
    )
    twist_sign = jnp.where(twist & ((lane_p == 0) | (lane_p == 3)), -1.0, 1.0)
    place = [
        jnp.where(fits & (source_p % 2 == part), twist_sign * (1.0 - 2.0 * part), 0.0).astype(BF16)
        for part in range(2)
    ]

    arrived(recv1, 0)
    coeffs = recv1[0]
    for chan in range(1, chans):
        coeffs = coeffs + recv1[chan]
    even = (iota(coeffs.shape, 1) // cycles) % 2 == 0
    real_block = jnp.where(even, coeffs, 0.0)
    imag_block = jnp.where(even, 0.0, -coeffs)
    spread = jnp.concatenate([real_block] * slots + [imag_block] * slots, axis=0).astype(BF16)
    stacked = dot(pick, spread, NT)
    own_block = (iota(stacked.shape, 1) // blks) % slots == iota(stacked.shape, 0) % slots
    stacked = jnp.where(own_block, stacked, 0.0).astype(BF16)

    piece = min(1024, width)
    grads = jnp.zeros((2 * half, 2 * slots), F32)
    for index in range(width // piece):
        window = pl.ds(index * piece, piece)
        table = phases[:, window]
        maps = dot(stacked, table, NN)
        weighted = (inv_v[:, window] * maps).astype(BF16)
        grads = grads + dot(table, weighted, NT)
    own_lane = (iota(grads.shape, 0) // blks) % slots == iota(grads.shape, 1) % slots
    grads = jnp.where(own_lane, grads, 0.0)
    placed = None
    for part in range(2):
        summed = grads[part * half : part * half + blks]
        for slot in range(1, slots):
            begin = part * half + slot * blks
            summed = summed + grads[begin : begin + blks]
        term = dot(summed.astype(BF16), place[part], NN)
        placed = term if placed is None else placed + term
    send2[...] = placed
    scatter(by_order, recv2, 1)
    sent(recv1, 0)

    arrived(recv2, 1)
    returned = recv2[0]
    for chan in range(1, chans):
        returned = returned + recv2[chan]
    lanes = returned.shape[1]
    blocks = [returned] + [
        pltpu.roll(returned, lanes - index * rows, 1) for index in range(1, 2 * slots)
    ]
    turned = jnp.concatenate(blocks, axis=0)[:, : max(rows, LANES)].T
    alm_grads = dot(turned[:rows].astype(BF16), slot_leg[...], NN) * gain_v[...]
    for comp in range(comps):
        mixed = mix_cols[0][comp] * alm_grads[0:8]
        for pair in range(1, chans // 2):
            mixed = mixed + mix_cols[pair][comp] * alm_grads[8 * pair : 8 * pair + 8]
        out_ref[comp] = mixed[0:4] + mixed[4:8]
    sent(recv2, 1)


def body(
    chans, blks, comp_alms, legendre, inv_noise, beam_window, mixing, channel_of, m_orders,
    cycle_of, cycle_pixels,
):
    comps, parts, order_dev, shard = comp_alms.shape
    cycles = legendre.shape[3]
    chan_dev, stokes, slots, width = inv_noise.shape
    assert parts == 4 and stokes == 2 and order_dev == 1 and chan_dev == 1
    rows = 4 * chans
    any_space = pl.BlockSpec(memory_space=pl.ANY)
    vector = pl.BlockSpec(memory_space=pltpu.VMEM)
    lanes2 = 2 * slots * rows
    assert lanes2 == 4 * cycles
    result = pl.pallas_call(
        functools.partial(kernel, chans, blks),
        out_shape=pltpu.VMEM((comps, 4, shard), F32),
        in_specs=[any_space] * 10,
        out_specs=vector,
        scratch_shapes=[
            pltpu.SMEM(mixing.shape, F32),
            pltpu.SMEM(channel_of.shape, jnp.int32),
            pltpu.SMEM(m_orders.shape, jnp.int32),
            pltpu.SMEM(cycle_of.shape, jnp.int32),
            pltpu.SMEM(cycle_pixels.shape, jnp.int32),
            pltpu.VMEM((1, cycles), jnp.int32),
            pltpu.VMEM((comps, 8, shard), F32),
            pltpu.VMEM((2, 4 * cycles, shard), BF16),
            pltpu.VMEM((2 * slots, width), F32),
            pltpu.VMEM((beam_window.shape[0], shard), F32),
            pltpu.VMEM((rows, shard), F32),
            pltpu.VMEM((2 * cycles, shard), BF16),
            pltpu.VMEM((2 * slots * blks, width), BF16),
            pltpu.VMEM((rows, 4 * cycles), F32),
            pltpu.VMEM((chans, blks, 4 * cycles), F32),
            pltpu.VMEM((blks, lanes2), F32),
            pltpu.VMEM((chans, blks, lanes2), F32),
            pltpu.VMEM((2, 1, 4 * cycles), F32),
            pltpu.SemaphoreType.DMA((10,)),
            pltpu.SemaphoreType.DMA((2,)),
            pltpu.SemaphoreType.DMA((2,)),
        ],
        compiler_params=pltpu.CompilerParams(collective_id=0, has_side_effects=True),
        name="normal_product",
    )(
        comp_alms, jnp.swapaxes(legendre, 2, 3), inv_noise, beam_window, mixing, channel_of,
        m_orders, cycle_of, cycle_pixels, cycle_of.reshape(1, cycles),
    )
    return result.reshape(comp_alms.shape)


def solution(mesh):
    in_specs = (
        P(None, None, "blk", "chan"),
        P(None, "blk", None, None),
        P("chan", None, "blk", None),
        P(),
        P(),
        P(),
        P(),
        P(),
        P(),
    )
    out_specs = P(None, None, "blk", "chan")
    work = functools.partial(body, mesh.shape["chan"], mesh.shape["blk"])
    return jax.shard_map(work, mesh=mesh, in_specs=in_specs, out_specs=out_specs, check_vma=False)
```

profile of v0, /device:TPU:0, one launch (start us, length us, event | category | flops | bytes accessed | tf_op | source)
XLA Modules:
  0.0 18.0 jit_solution(15040415871502460994)
XLA Ops:
  0.0 17.3 %normal_product.1 = f32[3,4,1024]{2,1,0:T(4,128)S(1)} custom-call(f32[3,4,1,1024]{3,2,1,0:T(1,128)} %alm_hbm.1, bf16[2,1,32,4096]{3,2,1,0:T(8,128)(2,1)} %bitcast.4, f32[1,2,4,8192]{3,2,1,0:T(4,128)} %inv_hbm.1, f32[4,4096]{1,0:T(4,128)} %beam_hbm.1, f32[4,3]{1,0:T(4,128)} %mix_hbm.1, s32[4]{0:T(128)} %chan_hbm.1, s32[8]{0:T(128)} %order_hbm.1, ...), custom_call_target="tpu_custom_call" | custom-call | tf_op jit(solution)/shard_map/normal_product/pallas_call | solution.py:310
  17.4 0.7 %copy.10 = f32[3,4,1,1024]{3,2,1,0:T(1,128)} copy(f32[3,4,1,1024]{3,1,0,2:T(4,128)S(1)} %bitcast.3) | data formatting | bytes 98304 | tf_op jit(solution)/shard_map/reshape | solution.py:344
where the time goes:
time: 18.2 us; the launch traced here: 18 us
  Pallas kernels  17.3 us (95%)
  local copies, waits for them, and re-layouts  0.67 us (4%)
    pallas_call x1, Pallas kernels, body(): pl.pallas_call(functools.partial(kernel, chans, blks), out_shape=pltpu.VM...  17.3 us
    reshape x1, local copies, waits for them, and re-layouts, body(): return result.reshape(comp_alms.shape)  0.67 us

commit v1 on v0

v1 whole, which is shorter than its diff:
```python
import functools
import math

import jax
import jax.numpy as jnp
from jax import lax
from jax.experimental import pallas as pl
from jax.experimental.pallas import tpu as pltpu
from jax.sharding import PartitionSpec as P

F32 = jnp.float32
BF16 = jnp.bfloat16
LANES = 128
NT = (((1,), (1,)), ((), ()))
NN = (((1,), (0,)), ((), ()))


def iota(shape, dim):
    return lax.broadcasted_iota(jnp.int32, shape, dim)


def dot(left, right, dims):
    return lax.dot_general(left, right, dims, preferred_element_type=F32)


def exact_mod(value, modulus, inverse):
    rest = value - jnp.floor(value * inverse) * modulus
    rest = jnp.where(rest < 0, rest + modulus, rest)
    return jnp.where(rest >= modulus, rest - modulus, rest)


def kernel(
    chans, blks, alm_hbm, leg_hbm, inv_hbm, beam_hbm, mix_hbm, chan_hbm, order_hbm, cycle_hbm,
    pixel_hbm, cycle_row_hbm, out_ref, mix_s, chan_s, order_s, cycle_s, pixel_s, cycle_row, comp_v,
    leg_v, inv_v, beam_v, gain_v, phases, fold_v, send1, recv1, send2, recv2, spare1, spare2, twin_v,
    in_sem, send_sem, recv_sem,
):
    comps = comp_v.shape[0]
    shard = comp_v.shape[2]
    cycles = leg_v.shape[1]
    slots = inv_v.shape[0] // 2
    width = inv_v.shape[1]
    rows = 4 * chans
    lanes = 4 * cycles
    total = chans * blks
    me_c = lax.axis_index("chan")
    me_b = lax.axis_index("blk")
    first = pl.multiple_of(me_c * shard, shard)

    def peer(offset):
        return lax.rem(me_c + offset // blks, chans), lax.rem(me_b + offset % blks, blks)

    def each_peer(act):
        if total <= 64:
            for offset in range(1, total):
                act(offset)
        else:
            lax.fori_loop(1, total, lambda offset, carry: (act(offset), carry)[1], 0)

    barrier = pltpu.get_barrier_semaphore()

    def greet(offset):
        pl.semaphore_signal(
            barrier, inc=1, device_id=peer(offset), device_id_type=pl.DeviceIdType.MESH
        )

    scalars = []

    def load(src, dst, group):
        copy = pltpu.make_async_copy(src, dst, in_sem.at[group])
        copy.start()
        return copy

    def loaded(dst, group):
        pltpu.make_async_copy(dst, dst, in_sem.at[group]).wait()

    for src, dst in (
        (order_hbm, order_s), (cycle_hbm, cycle_s), (pixel_hbm, pixel_s), (mix_hbm, mix_s),
        (chan_hbm, chan_s), (cycle_row_hbm, cycle_row),
    ):
        scalars.append(load(src, dst, 4 + len(scalars)))
    for kind in range(2):
        load(leg_hbm.at[kind, 0, :, pl.ds(first, shard)], leg_v.at[kind], 2)
    for comp in range(comps):
        for part in range(4):
            for half in range(2):
                load(alm_hbm.at[comp, part], comp_v.at[comp, pl.ds(4 * half + part, 1), :], 0)
    load(beam_hbm.at[:, pl.ds(first, shard)], beam_v, 1)
    for stokes in range(2):
        load(inv_hbm.at[0, stokes], inv_v.at[pl.ds(stokes * slots, slots), :], 3)
    each_peer(greet)
    for copy in scalars:
        copy.wait()

    own_cycles = [cycle_s[me_b * slots + slot] for slot in range(slots)]
    own_pixels = [pixel_s[cycle].astype(F32) for cycle in own_cycles]

    def by_slot(slot_index, values):
        result = jnp.where(slot_index == 0, values[0], values[slots - 1])
        for slot in range(1, slots - 1):
            result = jnp.where(slot_index == slot, values[slot], result)
        return result

    grid = (slots * blks, LANES)
    row = iota(grid, 0)
    lane = iota(grid, 1).astype(F32)
    pixels = by_slot(row // blks, own_pixels)
    orders = jnp.zeros(grid, F32)
    for order in range(blks):
        orders = jnp.where(row % blks == order, order_s[order].astype(F32), orders)
    modulus = 2.0 * pixels
    inverse = 1.0 / modulus
    scale = jnp.float32(math.pi) / pixels
    fine = exact_mod(orders * (2.0 * lane + 1.0), modulus, inverse) * scale
    stride = exact_mod(orders * (2.0 * LANES), modulus, inverse)
    coarse = exact_mod(stride * lane, modulus, inverse) * scale
    fine_cos, fine_sin = jnp.cos(fine), jnp.sin(fine)
    coarse_cos, coarse_sin = jnp.cos(coarse), jnp.sin(coarse)
    for chunk in range(width // LANES):
        window = pl.ds(chunk * LANES, LANES)
        turn_cos = coarse_cos[:, chunk : chunk + 1]
        turn_sin = coarse_sin[:, chunk : chunk + 1]
        real = turn_cos * fine_cos - turn_sin * fine_sin
        imag = turn_sin * fine_cos + turn_cos * fine_sin
        for slot in range(slots):
            own = slice(slot * blks, (slot + 1) * blks)
            both = jnp.concatenate([real[own], imag[own]], axis=0)
            phases[pl.ds(slot * 2 * blks, 2 * blks), window] = both.astype(BF16)

    loaded(comp_v, 0)
    loaded(beam_v, 1)
    loaded(leg_v, 2)
    low_half = iota((8, 1), 0) < 4
    keep = (iota((1, shard), 1) + first >= order_s[me_b]).astype(F32)
    alm_rows = []
    for pair in range(chans // 2):
        picked = [chan_s[2 * pair], chan_s[2 * pair + 1]]
        columns = [
            jnp.where(low_half, mix_s[picked[0], comp], mix_s[picked[1], comp])
            for comp in range(comps)
        ]
        mixed = columns[0] * comp_v[0]
        for comp in range(1, comps):
            mixed = mixed + columns[comp] * comp_v[comp]
        gains = [beam_v[pl.ds(chan, 1), :] * keep for chan in picked]
        gain_v[pl.ds(2 * pair, 1), :] = gains[0]
        gain_v[pl.ds(2 * pair + 1, 1), :] = gains[1]
        alm_rows.append(mixed * jnp.where(low_half, gains[0], gains[1]))
    alm = jnp.concatenate(alm_rows, axis=0).astype(BF16)
    plus = dot(alm, jnp.concatenate([leg_v[0]] * 4, axis=0), NT)
    minus = dot(alm, jnp.concatenate([leg_v[1]] * 4, axis=0), NT)
    row_part = iota(plus.shape, 0) % 4
    lane_part = iota(plus.shape, 1) // cycles
    outer = (lane_part == 0) | (lane_part == 3)
    signed = jnp.where(outer, -minus, minus)
    joined = jnp.where(lane_part == row_part, plus, 0.0) + jnp.where(
        lane_part == 3 - row_part, signed, 0.0
    )
    folded = joined
    for step in range(1, 4):
        folded = folded + pltpu.roll(joined, rows - step, 0)
    for chan in range(chans):
        send1[pl.ds(chan, 1), :] = folded[4 * chan : 4 * chan + 1]

    pl.semaphore_wait(barrier, total - 1)

    def scatter(src_of, dst_of, own_spare, phase):
        def start(offset):
            dest_c, dest_b = peer(offset)
            pltpu.make_async_remote_copy(
                src_ref=src_of(dest_b),
                dst_ref=dst_of(),
                send_sem=send_sem.at[phase],
                recv_sem=recv_sem.at[phase],
                device_id=(dest_c, dest_b),
                device_id_type=pl.DeviceIdType.MESH,
            ).start()

        each_peer(start)
        pltpu.make_async_copy(src_of(me_b), dst_of(), recv_sem.at[phase]).start()
        pltpu.make_async_copy(src_of(me_b), own_spare, send_sem.at[phase]).start()

    def arrived(dst, phase):
        pltpu.make_async_copy(dst, dst, recv_sem.at[phase]).wait()

    def sent(dst, phase):
        pltpu.make_async_copy(dst, dst, send_sem.at[phase]).wait()

    scatter(lambda dest_b: send1, lambda: recv1.at[me_c, me_b], spare1, 0)

    loaded(inv_v, 3)
    grid = (2 * slots, width)
    live = iota(grid, 1).astype(F32) < by_slot(iota((2 * slots, 1), 0) % slots, own_pixels)
    inv_v[...] = jnp.where(live, inv_v[...], 0.0)
    piece = min(1024, width)
    gram = None
    for index in range(width // piece):
        window = pl.ds(index * piece, piece)
        table = phases[:, window]
        blocks = []
        for slot in range(slots):
            for stokes in range(2):
                noise = inv_v[pl.ds(stokes * slots + slot, 1), window]
                wide = jnp.broadcast_to(noise, (2 * blks, piece)).astype(BF16)
                blocks.append(wide * table[slot * 2 * blks : (slot + 1) * 2 * blks])
        term = dot(table, jnp.concatenate(blocks, axis=0), NT)
        gram = term if gram is None else gram + term
    out_row = iota((2 * blks, lanes), 0)
    out_lane = iota((2 * blks, lanes), 1)
    lane_slot = out_lane // (4 * blks)
    picked_gram = gram[0 : 2 * blks]
    for slot in range(1, slots):
        picked_gram = jnp.where(
            lane_slot == slot, gram[slot * 2 * blks : (slot + 1) * 2 * blks], picked_gram
        )
    odd = (out_row // blks) != ((out_lane // blks) % 2)
    weight = 1.0 / by_slot(lane_slot, own_pixels)
    picked_gram = picked_gram * jnp.where(odd, -weight, weight)
    send2[0] = picked_gram[0:blks]
    send2[1] = picked_gram[blks : 2 * blks]
    scatter(
        lambda dest_b: send2.at[:, dest_b, :],
        lambda: recv2.at[me_b, pl.ds(2 * me_c, 2), :],
        spare2,
        1,
    )

    to_lane = iota((cycles, lanes), 1)
    spread = (
        iota((cycles, lanes), 0) == (to_lane % blks) * slots + to_lane // (4 * blks)
    ).astype(F32).astype(BF16)
    lane_cycle = dot(
        jnp.broadcast_to(cycle_row[...].astype(F32), (8, cycles)).astype(BF16), spread, NN
    )[0:1]
    from_row = iota((lanes, lanes), 0)
    square_lane = iota((lanes, lanes), 1)
    shuffle = (
        ((from_row % cycles).astype(F32) == lane_cycle)
        & (from_row // cycles == (square_lane // blks) % 4)
    ).astype(F32)
    leg_stack = jnp.concatenate([leg_v[0], leg_v[1]] * 2, axis=0)
    back_leg = dot(shuffle.T.astype(BF16), leg_stack, NN).astype(BF16)
    shuffle = shuffle.astype(BF16)

    arrived(recv1, 0)
    gathered = []
    for order in range(blks):
        coeffs = recv1[0, order]
        for chan in range(1, chans):
            coeffs = coeffs + recv1[chan, order]
        gathered.append(coeffs)
    coeffs = dot(jnp.concatenate(gathered, axis=0).astype(BF16), shuffle, NN)
    for order in range(blks):
        own = coeffs[order * chans : (order + 1) * chans]
        for tile in range(lanes // LANES):
            for part in range(2):
                twin_v[order, tile, pl.ds(part, chans, stride=2), :] = own[
                    :, tile * LANES : (tile + 1) * LANES
                ]
    turned = [
        jnp.concatenate([twin_v[order, tile] for tile in range(lanes // LANES)], axis=1)
        for order in range(blks)
    ]
    low_lane = iota((2 * chans, lanes), 1) % blks
    step = 1
    while step < blks:
        upper = (low_lane // step) % 2 == 1
        following = list(turned)
        for order in range(blks):
            if (order // step) % 2 == 0:
                one, two = turned[order], turned[order + step]
                following[order] = jnp.where(upper, pltpu.roll(two, step, 1), one)
                following[order + step] = jnp.where(
                    upper, two, pltpu.roll(one, lanes - step, 1)
                )
        turned = following
        step *= 2

    final_row = iota((8, lanes), 0)
    final_lane = iota((8, lanes), 1)
    row_real = final_row % 2
    row_stokes = (final_row // 2) % 2
    lane_kind = (final_lane // blks) % 2
    lane_stokes = (final_lane // (2 * blks)) % 2
    straight = (lane_kind == 0) & (lane_stokes == row_stokes)
    crossed = (lane_kind == 1) & (lane_stokes != row_stokes)
    cross_sign = jnp.where(row_stokes == row_real, -1.0, 1.0)
    mask = [
        jnp.where(straight & (row_real == real), 1.0, 0.0)
        + jnp.where(crossed & (row_real != real), cross_sign, 0.0)
        for real in range(2)
    ]

    arrived(recv2, 1)
    sums = [recv2[block] * turned[block] for block in range(blks)]
    step = blks // 2
    while step >= 1:
        upper = (low_lane // step) % 2 == 1
        merged = []
        for block in range(step):
            one, two = sums[block], sums[block + step]
            kept = jnp.where(upper, two, one)
            moved = jnp.where(upper, one, two)
            merged.append(
                kept
                + jnp.where(
                    upper, pltpu.roll(moved, step, 1), pltpu.roll(moved, lanes - step, 1)
                )
            )
        sums = merged
        step //= 2
    total_sum = sums[0]
    odd_part = (iota(total_sum.shape, 1) // blks) % 2 == 1
    total_sum = total_sum + jnp.where(
        odd_part, pltpu.roll(total_sum, blks, 1), pltpu.roll(total_sum, lanes - blks, 1)
    )
    total_sum = total_sum.astype(BF16).astype(F32)
    left = jnp.concatenate(
        [
            mask[0] * total_sum[2 * chan : 2 * chan + 1]
            + mask[1] * total_sum[2 * chan + 1 : 2 * chan + 2]
            for chan in range(chans)
        ],
        axis=0,
    )
    alm_grads = dot(left.astype(BF16), back_leg, NN)
    scaled = [
        alm_grads[8 * chan : 8 * chan + 8] * gain_v[pl.ds(chan, 1), :] for chan in range(chans)
    ]
    for comp in range(comps):
        mixed = mix_s[chan_s[0], comp] * scaled[0]
        for chan in range(1, chans):
            mixed = mixed + mix_s[chan_s[chan], comp] * scaled[chan]
        out_ref[comp] = mixed[0:4]
    sent(recv1, 0)
    sent(recv2, 1)


def body(
    chans, blks, comp_alms, legendre, inv_noise, beam_window, mixing, channel_of, m_orders,
    cycle_of, cycle_pixels,
):
    comps, parts, order_dev, shard = comp_alms.shape
    cycles = legendre.shape[3]
    chan_dev, stokes, slots, width = inv_noise.shape
    assert parts == 4 and stokes == 2 and order_dev == 1 and chan_dev == 1
    lanes = 4 * cycles
    assert slots * blks == cycles
    any_space = pl.BlockSpec(memory_space=pl.ANY)
    vector = pl.BlockSpec(memory_space=pltpu.VMEM)
    result = pl.pallas_call(
        functools.partial(kernel, chans, blks),
        out_shape=pltpu.VMEM((comps, 4, shard), F32),
        in_specs=[any_space] * 10,
        out_specs=vector,
        scratch_shapes=[
            pltpu.SMEM(mixing.shape, F32),
            pltpu.SMEM(channel_of.shape, jnp.int32),
            pltpu.SMEM(m_orders.shape, jnp.int32),
            pltpu.SMEM(cycle_of.shape, jnp.int32),
            pltpu.SMEM(cycle_pixels.shape, jnp.int32),
            pltpu.VMEM((1, cycles), jnp.int32),
            pltpu.VMEM((comps, 8, shard), F32),
            pltpu.VMEM((2, cycles, shard), BF16),
            pltpu.VMEM((2 * slots, width), F32),
            pltpu.VMEM((beam_window.shape[0], shard), F32),
            pltpu.VMEM((chans, shard), F32),
            pltpu.VMEM((2 * slots * blks, width), BF16),
            pltpu.VMEM((4 * chans, lanes), F32),
            pltpu.VMEM((chans, lanes), F32),
            pltpu.VMEM((chans, blks, chans, lanes), F32),
            pltpu.VMEM((2, blks, lanes), F32),
            pltpu.VMEM((blks, 2 * chans, lanes), F32),
            pltpu.VMEM((chans, lanes), F32),
            pltpu.VMEM((2, lanes), F32),
            pltpu.VMEM((blks, lanes // LANES, 2 * chans, LANES), F32),
            pltpu.SemaphoreType.DMA((10,)),
            pltpu.SemaphoreType.DMA((2,)),
            pltpu.SemaphoreType.DMA((2,)),
        ],
        compiler_params=pltpu.CompilerParams(collective_id=0, has_side_effects=True),
        name="normal_product",
    )(
        comp_alms, jnp.swapaxes(legendre, 2, 3), inv_noise, beam_window, mixing, channel_of,
        m_orders, cycle_of, cycle_pixels, cycle_of.reshape(1, cycles),
    )
    return result.reshape(comp_alms.shape)


def solution(mesh):
    in_specs = (
        P(None, None, "blk", "chan"),
        P(None, "blk", None, None),
        P("chan", None, "blk", None),
        P(),
        P(),
        P(),
        P(),
        P(),
        P(),
    )
    out_specs = P(None, None, "blk", "chan")
    work = functools.partial(body, mesh.shape["chan"], mesh.shape["blk"])
    return jax.shard_map(work, mesh=mesh, in_specs=in_specs, out_specs=out_specs, check_vma=False)
```

time: 18.2 us -> 13.2 us (0.73)
  Pallas kernels: 17.3 us -> 12.4 us
    pallas_call x1, Pallas kernels: 17.3 us -> 12.4 us  [body(): pl.pallas_call(functools.partial(kernel, chans, blks), out_shape=pltpu.VM...]
where the time goes in v1:
time: 13.2 us; the launch traced here: 13.1 us
  Pallas kernels  12.4 us (94%)
  local copies, waits for them, and re-layouts  0.67 us (5%)
    pallas_call x1, Pallas kernels, body(): pl.pallas_call(functools.partial(kernel, chans, blks), out_shape=pltpu.VM...  12.4 us
    reshape x1, local copies, waits for them, and re-layouts, body(): return result.reshape(comp_alms.shape)  0.67 us

profile of v1, /device:TPU:0, one launch (start us, length us, event | category | flops | bytes accessed | tf_op | source)
XLA Modules:
  0.0 13.1 jit_solution(8993427107362820686)
XLA Ops:
  0.0 12.4 %normal_product.1 = f32[3,4,1024]{2,1,0:T(4,128)S(1)} custom-call(f32[3,4,1,1024]{3,2,1,0:T(1,128)} %alm_hbm.1, bf16[2,1,32,4096]{3,2,1,0:T(8,128)(2,1)} %bitcast.4, f32[1,2,4,8192]{3,2,1,0:T(4,128)} %inv_hbm.1, f32[4,4096]{1,0:T(4,128)} %beam_hbm.1, f32[4,3]{1,0:T(4,128)} %mix_hbm.1, s32[4]{0:T(128)} %chan_hbm.1, s32[8]{0:T(128)} %order_hbm.1, ...), custom_call_target="tpu_custom_call" | custom-call | tf_op jit(solution)/shard_map/normal_product/pallas_call | solution.py:351
  12.4 0.7 %copy.10 = f32[3,4,1,1024]{3,2,1,0:T(1,128)} copy(f32[3,4,1,1024]{3,1,0,2:T(4,128)S(1)} %bitcast.3) | data formatting | bytes 98304 | tf_op jit(solution)/shard_map/reshape | solution.py:387

commit v2 on v1

--- a/solution.py
+++ b/solution.py
@@ -29,17 +29,43 @@
     return jnp.where(rest >= modulus, rest - modulus, rest)
 
 
+def turn(steps, count, double_inverse):
+    quarter = jnp.floor(steps * double_inverse + 0.5)
+    angle = (2.0 * steps - quarter * count) * (double_inverse * jnp.float32(math.pi / 4))
+    square = angle * angle
+    sine = angle + angle * square * (
+        (-1.9515295891e-4 * square + 8.3321608736e-3) * square - 1.6666654611e-1
+    )
+    cosine = (1.0 - 0.5 * square) + square * square * (
+        (2.443315711809948e-5 * square - 1.388731625493765e-3) * square + 4.166664568298827e-2
+    )
+    index = quarter.astype(jnp.int32)
+    odd = index % 2 == 1
+    real = jnp.where(odd, sine, cosine)
+    imag = jnp.where(odd, cosine, sine)
+    real = jnp.where((index + 1) // 2 % 2 == 1, -real, real)
+    imag = jnp.where(index // 2 % 2 == 1, -imag, imag)
+    return real, imag
+
+
+def pair_turns(cosines, sines, order):
+    cos_one, sin_one = cosines[order : order + 1], sines[order : order + 1]
+    cos_cos, sin_sin = cos_one * cosines, sin_one * sines
+    sin_cos, cos_sin = sin_one * cosines, cos_one * sines
+    return [cos_cos - sin_sin, sin_cos + cos_sin, cos_cos + sin_sin, sin_cos - cos_sin]
+
+
 def kernel(
     chans, blks, alm_hbm, leg_hbm, inv_hbm, beam_hbm, mix_hbm, chan_hbm, order_hbm, cycle_hbm,
     pixel_hbm, cycle_row_hbm, out_ref, mix_s, chan_s, order_s, cycle_s, pixel_s, cycle_row, comp_v,
-    leg_v, inv_v, beam_v, gain_v, phases, fold_v, send1, recv1, send2, recv2, spare1, spare2, twin_v,
+    leg_v, inv_v, beam_v, gain_v, fine_v, coarse_v, send1, recv1, send2, recv2, spare1, spare2, twin_v,
     in_sem, send_sem, recv_sem,
 ):
     comps = comp_v.shape[0]
     shard = comp_v.shape[2]
     cycles = leg_v.shape[1]
-    slots = inv_v.shape[0] // 2
-    width = inv_v.shape[1]
+    slots = inv_v.shape[0]
+    chunks = inv_v.shape[1] // 2
     rows = 4 * chans
     lanes = 4 * cycles
     total = chans * blks
@@ -87,7 +113,12 @@
                 load(alm_hbm.at[comp, part], comp_v.at[comp, pl.ds(4 * half + part, 1), :], 0)
     load(beam_hbm.at[:, pl.ds(first, shard)], beam_v, 1)
     for stokes in range(2):
-        load(inv_hbm.at[0, stokes], inv_v.at[pl.ds(stokes * slots, slots), :], 3)
+        for slot in range(slots):
+            load(
+                inv_hbm.at[stokes, :, slot, :],
+                inv_v.at[slot, pl.ds(stokes * chunks, chunks), :],
+                3,
+            )
     each_peer(greet)
     for copy in scalars:
         copy.wait()
@@ -109,23 +140,25 @@
     for order in range(blks):
         orders = jnp.where(row % blks == order, order_s[order].astype(F32), orders)
     modulus = 2.0 * pixels
-    inverse = 1.0 / modulus
-    scale = jnp.float32(math.pi) / pixels
-    fine = exact_mod(orders * (2.0 * lane + 1.0), modulus, inverse) * scale
+    reciprocal = 1.0 / pixels
+    inverse = 0.5 * reciprocal
+    double_inverse = 2.0 * reciprocal
+    chunk = (iota(grid, 1) % chunks).astype(F32)
+    fine = exact_mod(orders * (2.0 * lane + 1.0), modulus, inverse)
     stride = exact_mod(orders * (2.0 * LANES), modulus, inverse)
-    coarse = exact_mod(stride * lane, modulus, inverse) * scale
-    fine_cos, fine_sin = jnp.cos(fine), jnp.sin(fine)
-    coarse_cos, coarse_sin = jnp.cos(coarse), jnp.sin(coarse)
-    for chunk in range(width // LANES):
-        window = pl.ds(chunk * LANES, LANES)
-        turn_cos = coarse_cos[:, chunk : chunk + 1]
-        turn_sin = coarse_sin[:, chunk : chunk + 1]
-        real = turn_cos * fine_cos - turn_sin * fine_sin
-        imag = turn_sin * fine_cos + turn_cos * fine_sin
-        for slot in range(slots):
-            own = slice(slot * blks, (slot + 1) * blks)
-            both = jnp.concatenate([real[own], imag[own]], axis=0)
-            phases[pl.ds(slot * 2 * blks, 2 * blks), window] = both.astype(BF16)
+    coarse = exact_mod(stride * chunk, modulus, inverse)
+    fine_cos, fine_sin = turn(fine, pixels, double_inverse)
+    coarse_cos, coarse_sin = turn(coarse, pixels, double_inverse)
+    for slot in range(slots):
+        own = slice(slot * blks, (slot + 1) * blks)
+        for order in range(blks):
+            block = pl.ds(order * 4 * blks, 4 * blks)
+            fine_v[slot, block, :] = jnp.concatenate(
+                pair_turns(fine_cos[own], fine_sin[own], order), axis=0
+            ).astype(BF16)
+            coarse_v[slot, block, :] = jnp.concatenate(
+                pair_turns(coarse_cos[own], coarse_sin[own], order), axis=0
+            )
 
     loaded(comp_v, 0)
     loaded(beam_v, 1)
@@ -189,37 +222,41 @@
     scatter(lambda dest_b: send1, lambda: recv1.at[me_c, me_b], spare1, 0)
 
     loaded(inv_v, 3)
-    grid = (2 * slots, width)
-    live = iota(grid, 1).astype(F32) < by_slot(iota((2 * slots, 1), 0) % slots, own_pixels)
-    inv_v[...] = jnp.where(live, inv_v[...], 0.0)
-    piece = min(1024, width)
-    gram = None
-    for index in range(width // piece):
-        window = pl.ds(index * piece, piece)
-        table = phases[:, window]
-        blocks = []
-        for slot in range(slots):
-            for stokes in range(2):
-                noise = inv_v[pl.ds(stokes * slots + slot, 1), window]
-                wide = jnp.broadcast_to(noise, (2 * blks, piece)).astype(BF16)
-                blocks.append(wide * table[slot * 2 * blks : (slot + 1) * 2 * blks])
-        term = dot(table, jnp.concatenate(blocks, axis=0), NT)
-        gram = term if gram is None else gram + term
-    out_row = iota((2 * blks, lanes), 0)
-    out_lane = iota((2 * blks, lanes), 1)
-    lane_slot = out_lane // (4 * blks)
-    picked_gram = gram[0 : 2 * blks]
-    for slot in range(1, slots):
-        picked_gram = jnp.where(
-            lane_slot == slot, gram[slot * 2 * blks : (slot + 1) * 2 * blks], picked_gram
-        )
-    odd = (out_row // blks) != ((out_lane // blks) % 2)
-    weight = 1.0 / by_slot(lane_slot, own_pixels)
-    picked_gram = picked_gram * jnp.where(odd, -weight, weight)
-    send2[0] = picked_gram[0:blks]
-    send2[1] = picked_gram[blks : 2 * blks]
+    grid = (2 * chunks, LANES)
+    pixel_index = (iota(grid, 0) % chunks) * LANES + iota(grid, 1)
+    parts = [[] for _ in range(blks)]
+    for slot in range(slots):
+        live = pixel_index.astype(F32) < own_pixels[slot]
+        noise = jnp.where(live, inv_v[slot], 0.0).astype(BF16)
+        inner = dot(fine_v[slot], noise, NT)
+        for order in range(blks):
+            base = order * 4 * blks
+            held = [inner[base + kind * blks : base + (kind + 1) * blks] for kind in range(4)]
+            outer_turn = [
+                coarse_v[slot, pl.ds(base + kind * blks, blks), :] for kind in range(4)
+            ]
+            add_real = outer_turn[0] * held[0] - outer_turn[1] * held[1]
+            add_imag = outer_turn[0] * held[1] + outer_turn[1] * held[0]
+            sub_real = outer_turn[2] * held[2] - outer_turn[3] * held[3]
+            sub_imag = outer_turn[2] * held[3] + outer_turn[3] * held[2]
+            parts[order].append(
+                jnp.concatenate(
+                    [
+                        sub_real + add_real,
+                        sub_imag - add_imag,
+                        -sub_imag - add_imag,
+                        sub_real - add_real,
+                    ],
+                    axis=0,
+                ).astype(BF16)
+            )
+    ones = (iota((8, LANES), 1) // chunks == iota((8, LANES), 0)).astype(F32).astype(BF16)
+    weight = 0.5 / by_slot(iota((2, lanes), 1) // (4 * blks), own_pixels)
+    for order in range(blks):
+        summed = dot(ones, jnp.concatenate(parts[order], axis=0), NT)
+        send2[order] = summed[0:2] * weight
     scatter(
-        lambda dest_b: send2.at[:, dest_b, :],
+        lambda dest_b: send2.at[dest_b],
         lambda: recv2.at[me_b, pl.ds(2 * me_c, 2), :],
         spare2,
         1,
@@ -232,15 +269,22 @@
     lane_cycle = dot(
         jnp.broadcast_to(cycle_row[...].astype(F32), (8, cycles)).astype(BF16), spread, NN
     )[0:1]
-    from_row = iota((lanes, lanes), 0)
-    square_lane = iota((lanes, lanes), 1)
+    half = (2 * cycles, lanes)
+    from_row = iota(half, 0)
     shuffle = (
         ((from_row % cycles).astype(F32) == lane_cycle)
-        & (from_row // cycles == (square_lane // blks) % 4)
+        & (from_row // cycles == (iota(half, 1) // blks) % 2)
     ).astype(F32)
-    leg_stack = jnp.concatenate([leg_v[0], leg_v[1]] * 2, axis=0)
+    leg_stack = jnp.concatenate([leg_v[0], leg_v[1]], axis=0)
     back_leg = dot(shuffle.T.astype(BF16), leg_stack, NN).astype(BF16)
-    shuffle = shuffle.astype(BF16)
+    empty = jnp.zeros(half, F32)
+    shuffle = jnp.concatenate(
+        [
+            jnp.concatenate([shuffle, empty], axis=1),
+            jnp.concatenate([empty, shuffle], axis=1),
+        ],
+        axis=0,
+    ).astype(BF16)
 
     arrived(recv1, 0)
     gathered = []
@@ -254,8 +298,9 @@
         own = coeffs[order * chans : (order + 1) * chans]
         for tile in range(lanes // LANES):
             for part in range(2):
+                begin = part * lanes + tile * LANES
                 twin_v[order, tile, pl.ds(part, chans, stride=2), :] = own[
-                    :, tile * LANES : (tile + 1) * LANES
+                    :, begin : begin + LANES
                 ]
     turned = [
         jnp.concatenate([twin_v[order, tile] for tile in range(lanes // LANES)], axis=1)
@@ -281,14 +326,14 @@
     row_real = final_row % 2
     row_stokes = (final_row // 2) % 2
     lane_kind = (final_lane // blks) % 2
-    lane_stokes = (final_lane // (2 * blks)) % 2
-    straight = (lane_kind == 0) & (lane_stokes == row_stokes)
-    crossed = (lane_kind == 1) & (lane_stokes != row_stokes)
+    lane_real = (final_lane // (2 * blks)) % 2
+    straight = (lane_kind == 0) & (lane_real == row_real)
+    crossed = (lane_kind == 1) & (lane_real != row_real)
     cross_sign = jnp.where(row_stokes == row_real, -1.0, 1.0)
     mask = [
-        jnp.where(straight & (row_real == real), 1.0, 0.0)
-        + jnp.where(crossed & (row_real != real), cross_sign, 0.0)
-        for real in range(2)
+        jnp.where(straight & (row_stokes == stokes), 1.0, 0.0)
+        + jnp.where(crossed & (row_stokes != stokes), cross_sign, 0.0)
+        for stokes in range(2)
     ]
 
     arrived(recv2, 1)
@@ -346,6 +391,9 @@
     assert parts == 4 and stokes == 2 and order_dev == 1 and chan_dev == 1
     lanes = 4 * cycles
     assert slots * blks == cycles
+    chunks = width // LANES
+    assert 2 * chunks == LANES
+    noise = jnp.swapaxes(inv_noise.reshape(stokes, slots, chunks, LANES), 1, 2)
     any_space = pl.BlockSpec(memory_space=pl.ANY)
     vector = pl.BlockSpec(memory_space=pltpu.VMEM)
     result = pl.pallas_call(
@@ -362,14 +410,14 @@
             pltpu.VMEM((1, cycles), jnp.int32),
             pltpu.VMEM((comps, 8, shard), F32),
             pltpu.VMEM((2, cycles, shard), BF16),
-            pltpu.VMEM((2 * slots, width), F32),
+            pltpu.VMEM((slots, 2 * chunks, LANES), F32),
             pltpu.VMEM((beam_window.shape[0], shard), F32),
             pltpu.VMEM((chans, shard), F32),
-            pltpu.VMEM((2 * slots * blks, width), BF16),
-            pltpu.VMEM((4 * chans, lanes), F32),
+            pltpu.VMEM((slots, 4 * blks * blks, LANES), BF16),
+            pltpu.VMEM((slots, 4 * blks * blks, LANES), F32),
             pltpu.VMEM((chans, lanes), F32),
             pltpu.VMEM((chans, blks, chans, lanes), F32),
-            pltpu.VMEM((2, blks, lanes), F32),
+            pltpu.VMEM((blks, 2, lanes), F32),
             pltpu.VMEM((blks, 2 * chans, lanes), F32),
             pltpu.VMEM((chans, lanes), F32),
             pltpu.VMEM((2, lanes), F32),
@@ -381,7 +429,7 @@
         compiler_params=pltpu.CompilerParams(collective_id=0, has_side_effects=True),
         name="normal_product",
     )(
-        comp_alms, jnp.swapaxes(legendre, 2, 3), inv_noise, beam_window, mixing, channel_of,
+        comp_alms, jnp.swapaxes(legendre, 2, 3), noise, beam_window, mixing, channel_of,
         m_orders, cycle_of, cycle_pixels, cycle_of.reshape(1, cycles),
     )
     return result.reshape(comp_alms.shape)

time: 13.2 us -> 12.2 us (0.924)
  Pallas kernels: 12.4 us -> 11.3 us
    pallas_call x1, Pallas kernels: 12.4 us -> 11.3 us  [body(): pl.pallas_call(functools.partial(kernel, chans, blks), out_shape=pltpu.VM...]
where the time goes in v2:
time: 12.2 us; the launch traced here: 12 us
  Pallas kernels  11.3 us (93%)
  local copies, waits for them, and re-layouts  0.67 us (5%)
    pallas_call x1, Pallas kernels, body(): pl.pallas_call(functools.partial(kernel, chans, blks), out_shape=pltpu.VM...  11.3 us
    reshape x1, local copies, waits for them, and re-layouts, body(): return result.reshape(comp_alms.shape)  0.67 us

profile of v2, /device:TPU:0, one launch (start us, length us, event | category | flops | bytes accessed | tf_op | source)
XLA Modules:
  0.0 12.0 jit_solution(8394138579618242610)
XLA Ops:
  0.0 11.3 %normal_product.1 = f32[3,4,1024]{2,1,0:T(4,128)S(1)} custom-call(f32[3,4,1,1024]{3,2,1,0:T(1,128)} %alm_hbm.1, bf16[2,1,32,4096]{3,2,1,0:T(8,128)(2,1)} %bitcast.7, f32[2,64,4,128]{3,2,1,0:T(4,128)} %bitcast.8, f32[4,4096]{1,0:T(4,128)} %beam_hbm.1, f32[4,3]{1,0:T(4,128)} %mix_hbm.1, s32[4]{0:T(128)} %chan_hbm.1, s32[8]{0:T(128)} %order_hbm.1, ...), custom_call_target="tpu_custom_call" | custom-call | tf_op jit(solution)/shard_map/normal_product/pallas_call | solution.py:399
  11.3 0.7 %copy.10 = f32[3,4,1,1024]{3,2,1,0:T(1,128)} copy(f32[3,4,1,1024]{3,1,0,2:T(4,128)S(1)} %bitcast.6) | data formatting | bytes 98304 | tf_op jit(solution)/shard_map/reshape | solution.py:435

commit v3 on v2

--- a/solution.py
+++ b/solution.py
@@ -23,10 +23,14 @@
     return lax.dot_general(left, right, dims, preferred_element_type=F32)
 
 
-def exact_mod(value, modulus, inverse):
-    rest = value - jnp.floor(value * inverse) * modulus
-    rest = jnp.where(rest < 0, rest + modulus, rest)
-    return jnp.where(rest >= modulus, rest - modulus, rest)
+def rest(value, size):
+    return value & (size - 1) if size & (size - 1) == 0 else lax.rem(value, jnp.int32(size))
+
+
+def share(value, size):
+    if size & (size - 1) == 0:
+        return value >> (size.bit_length() - 1)
+    return lax.div(value, jnp.int32(size))
 
 
 def turn(steps, count, double_inverse):
@@ -40,11 +44,11 @@
         (2.443315711809948e-5 * square - 1.388731625493765e-3) * square + 4.166664568298827e-2
     )
     index = quarter.astype(jnp.int32)
-    odd = index % 2 == 1
+    odd = (index & 1) == 1
     real = jnp.where(odd, sine, cosine)
     imag = jnp.where(odd, cosine, sine)
-    real = jnp.where((index + 1) // 2 % 2 == 1, -real, real)
-    imag = jnp.where(index // 2 % 2 == 1, -imag, imag)
+    real = jnp.where(((index + 1) & 2) == 2, -real, real)
+    imag = jnp.where((index & 2) == 2, -imag, imag)
     return real, imag
 
 
@@ -73,21 +77,29 @@
     me_b = lax.axis_index("blk")
     first = pl.multiple_of(me_c * shard, shard)
 
+    me = me_b * chans + me_c
+
     def peer(offset):
-        return lax.rem(me_c + offset // blks, chans), lax.rem(me_b + offset % blks, blks)
-
-    def each_peer(act):
-        if total <= 64:
-            for offset in range(1, total):
+        index = offset - 1 + (me < offset).astype(jnp.int32)
+        return lax.rem(index, chans), index // chans
+
+    def each(first_offset, last_offset, act):
+        if last_offset - first_offset <= 64:
+            for offset in range(first_offset, last_offset):
                 act(offset)
         else:
-            lax.fori_loop(1, total, lambda offset, carry: (act(offset), carry)[1], 0)
+            lax.fori_loop(
+                first_offset, last_offset, lambda offset, carry: (act(offset), carry)[1], 0
+            )
 
     barrier = pltpu.get_barrier_semaphore()
 
-    def greet(offset):
+    def tell(semaphore, dest_c, dest_b):
         pl.semaphore_signal(
-            barrier, inc=1, device_id=peer(offset), device_id_type=pl.DeviceIdType.MESH
+            semaphore,
+            inc=1,
+            device_id=(dest_c, dest_b),
+            device_id_type=pl.DeviceIdType.MESH,
         )
 
     scalars = []
@@ -119,7 +131,13 @@
                 inv_v.at[slot, pl.ds(stokes * chunks, chunks), :],
                 3,
             )
-    each_peer(greet)
+    each(
+        1,
+        total,
+        lambda offset: tell(
+            barrier, lax.rem(me_c + offset // blks, chans), lax.rem(me_b + offset % blks, blks)
+        ),
+    )
     for copy in scalars:
         copy.wait()
 
@@ -132,33 +150,28 @@
             result = jnp.where(slot_index == slot, values[slot], result)
         return result
 
-    grid = (slots * blks, LANES)
+    grid = (blks, LANES)
     row = iota(grid, 0)
-    lane = iota(grid, 1).astype(F32)
-    pixels = by_slot(row // blks, own_pixels)
-    orders = jnp.zeros(grid, F32)
-    for order in range(blks):
-        orders = jnp.where(row % blks == order, order_s[order].astype(F32), orders)
-    modulus = 2.0 * pixels
-    reciprocal = 1.0 / pixels
-    inverse = 0.5 * reciprocal
-    double_inverse = 2.0 * reciprocal
-    chunk = (iota(grid, 1) % chunks).astype(F32)
-    fine = exact_mod(orders * (2.0 * lane + 1.0), modulus, inverse)
-    stride = exact_mod(orders * (2.0 * LANES), modulus, inverse)
-    coarse = exact_mod(stride * chunk, modulus, inverse)
-    fine_cos, fine_sin = turn(fine, pixels, double_inverse)
-    coarse_cos, coarse_sin = turn(coarse, pixels, double_inverse)
+    lane = iota(grid, 1)
+    orders = jnp.full(grid, order_s[0], jnp.int32)
+    for order in range(1, blks):
+        orders = jnp.where(row == order, order_s[order], orders)
+    orders = orders.astype(F32)
+    fine = orders * (2 * lane + 1).astype(F32)
+    leap = orders * (2.0 * LANES)
+    chunk = rest(lane, chunks).astype(F32)
     for slot in range(slots):
-        own = slice(slot * blks, (slot + 1) * blks)
+        pixels = jnp.full(grid, own_pixels[slot], F32)
+        reciprocal = 1.0 / pixels
+        stride = leap - jnp.floor(leap * (0.5 * reciprocal)) * (2.0 * pixels)
+        fine_turn = turn(fine, pixels, 2.0 * reciprocal)
+        coarse_turn = turn(stride * chunk, pixels, 2.0 * reciprocal)
         for order in range(blks):
             block = pl.ds(order * 4 * blks, 4 * blks)
             fine_v[slot, block, :] = jnp.concatenate(
-                pair_turns(fine_cos[own], fine_sin[own], order), axis=0
+                pair_turns(*fine_turn, order), axis=0
             ).astype(BF16)
-            coarse_v[slot, block, :] = jnp.concatenate(
-                pair_turns(coarse_cos[own], coarse_sin[own], order), axis=0
-            )
+            coarse_v[slot, block, :] = jnp.concatenate(pair_turns(*coarse_turn, order), axis=0)
 
     loaded(comp_v, 0)
     loaded(beam_v, 1)
@@ -195,23 +208,6 @@
     for chan in range(chans):
         send1[pl.ds(chan, 1), :] = folded[4 * chan : 4 * chan + 1]
 
-    pl.semaphore_wait(barrier, total - 1)
-
-    def scatter(src_of, dst_of, own_spare, phase):
-        def start(offset):
-            dest_c, dest_b = peer(offset)
-            pltpu.make_async_remote_copy(
-                src_ref=src_of(dest_b),
-                dst_ref=dst_of(),
-                send_sem=send_sem.at[phase],
-                recv_sem=recv_sem.at[phase],
-                device_id=(dest_c, dest_b),
-                device_id_type=pl.DeviceIdType.MESH,
-            ).start()
-
-        each_peer(start)
-        pltpu.make_async_copy(src_of(me_b), dst_of(), recv_sem.at[phase]).start()
-        pltpu.make_async_copy(src_of(me_b), own_spare, send_sem.at[phase]).start()
 
     def arrived(dst, phase):
         pltpu.make_async_copy(dst, dst, recv_sem.at[phase]).wait()
@@ -219,11 +215,30 @@
     def sent(dst, phase):
         pltpu.make_async_copy(dst, dst, send_sem.at[phase]).wait()
 
-    scatter(lambda dest_b: send1, lambda: recv1.at[me_c, me_b], spare1, 0)
-
+    def routes(dest_b):
+        return (
+            (send1, recv1.at[me_c, me_b]),
+            (send2.at[dest_b], recv2.at[me_b, pl.ds(2 * me_c, 2), :]),
+        )
+
+    def post(offset, phase):
+        dest_c, dest_b = peer(offset)
+        src, dst = routes(dest_b)[phase]
+        pltpu.make_async_remote_copy(
+            src_ref=src,
+            dst_ref=dst,
+            send_sem=send_sem.at[phase],
+            recv_sem=recv_sem.at[phase],
+            device_id=(dest_c, dest_b),
+            device_id_type=pl.DeviceIdType.MESH,
+        ).start()
+
+    early = min(4, total - 1)
+    pl.semaphore_wait(barrier, total - 1)
+    each(1, early + 1, lambda offset: post(offset, 0))
     loaded(inv_v, 3)
     grid = (2 * chunks, LANES)
-    pixel_index = (iota(grid, 0) % chunks) * LANES + iota(grid, 1)
+    pixel_index = rest(iota(grid, 0), chunks) * LANES + iota(grid, 1)
     parts = [[] for _ in range(blks)]
     for slot in range(slots):
         live = pixel_index.astype(F32) < own_pixels[slot]
@@ -250,21 +265,20 @@
                     axis=0,
                 ).astype(BF16)
             )
-    ones = (iota((8, LANES), 1) // chunks == iota((8, LANES), 0)).astype(F32).astype(BF16)
-    weight = 0.5 / by_slot(iota((2, lanes), 1) // (4 * blks), own_pixels)
+    ones = (share(iota((8, LANES), 1), chunks) == iota((8, LANES), 0)).astype(F32).astype(BF16)
+    weight = 0.5 / by_slot(share(iota((2, lanes), 1), 4 * blks), own_pixels)
     for order in range(blks):
         summed = dot(ones, jnp.concatenate(parts[order], axis=0), NT)
         send2[order] = summed[0:2] * weight
-    scatter(
-        lambda dest_b: send2.at[dest_b],
-        lambda: recv2.at[me_b, pl.ds(2 * me_c, 2), :],
-        spare2,
-        1,
-    )
+    each(1, early + 1, lambda offset: post(offset, 1))
+    each(early + 1, total, lambda offset: (post(offset, 0), post(offset, 1)))
+    for phase, (src, dst) in enumerate(routes(me_b)):
+        pltpu.make_async_copy(src, dst, recv_sem.at[phase]).start()
+        pltpu.make_async_copy(src, (spare1, spare2)[phase], send_sem.at[phase]).start()
 
     to_lane = iota((cycles, lanes), 1)
     spread = (
-        iota((cycles, lanes), 0) == (to_lane % blks) * slots + to_lane // (4 * blks)
+        iota((cycles, lanes), 0) == rest(to_lane, blks) * slots + share(to_lane, 4 * blks)
     ).astype(F32).astype(BF16)
     lane_cycle = dot(
         jnp.broadcast_to(cycle_row[...].astype(F32), (8, cycles)).astype(BF16), spread, NN
@@ -272,8 +286,8 @@
     half = (2 * cycles, lanes)
     from_row = iota(half, 0)
     shuffle = (
-        ((from_row % cycles).astype(F32) == lane_cycle)
-        & (from_row // cycles == (iota(half, 1) // blks) % 2)
+        (rest(from_row, cycles).astype(F32) == lane_cycle)
+        & (share(from_row, cycles) == (share(iota(half, 1), blks) & 1))
     ).astype(F32)
     leg_stack = jnp.concatenate([leg_v[0], leg_v[1]], axis=0)
     back_leg = dot(shuffle.T.astype(BF16), leg_stack, NN).astype(BF16)
@@ -306,10 +320,10 @@
         jnp.concatenate([twin_v[order, tile] for tile in range(lanes // LANES)], axis=1)
         for order in range(blks)
     ]
-    low_lane = iota((2 * chans, lanes), 1) % blks
+    low_lane = iota((2 * chans, lanes), 1)
     step = 1
     while step < blks:
-        upper = (low_lane // step) % 2 == 1
+        upper = (share(low_lane, step) & 1) == 1
         following = list(turned)
         for order in range(blks):
             if (order // step) % 2 == 0:
@@ -323,10 +337,10 @@
 
     final_row = iota((8, lanes), 0)
     final_lane = iota((8, lanes), 1)
-    row_real = final_row % 2
-    row_stokes = (final_row // 2) % 2
-    lane_kind = (final_lane // blks) % 2
-    lane_real = (final_lane // (2 * blks)) % 2
+    row_real = final_row & 1
+    row_stokes = (final_row >> 1) & 1
+    lane_kind = share(final_lane, blks) & 1
+    lane_real = share(final_lane, 2 * blks) & 1
     straight = (lane_kind == 0) & (lane_real == row_real)
     crossed = (lane_kind == 1) & (lane_real != row_real)
     cross_sign = jnp.where(row_stokes == row_real, -1.0, 1.0)
@@ -340,7 +354,7 @@
     sums = [recv2[block] * turned[block] for block in range(blks)]
     step = blks // 2
     while step >= 1:
-        upper = (low_lane // step) % 2 == 1
+        upper = (share(low_lane, step) & 1) == 1
         merged = []
         for block in range(step):
             one, two = sums[block], sums[block + step]
@@ -355,7 +369,7 @@
         sums = merged
         step //= 2
     total_sum = sums[0]
-    odd_part = (iota(total_sum.shape, 1) // blks) % 2 == 1
+    odd_part = (share(iota(total_sum.shape, 1), blks) & 1) == 1
     total_sum = total_sum + jnp.where(
         odd_part, pltpu.roll(total_sum, blks, 1), pltpu.roll(total_sum, lanes - blks, 1)
     )

time: 12.2 us -> 11.6 us (0.951)
  Pallas kernels: 11.3 us -> 10.8 us
    pallas_call x1, Pallas kernels: 11.3 us -> 10.8 us  [body(): pl.pallas_call(functools.partial(kernel, chans, blks), out_shape=pltpu.VM...]
where the time goes in v3:
time: 11.6 us; the launch traced here: 11.5 us
  Pallas kernels  10.8 us (93%)
  local copies, waits for them, and re-layouts  0.67 us (6%)
    pallas_call x1, Pallas kernels, body(): pl.pallas_call(functools.partial(kernel, chans, blks), out_shape=pltpu.VM...  10.8 us
    reshape x1, local copies, waits for them, and re-layouts, body(): return result.reshape(comp_alms.shape)  0.67 us

profile of v3, /device:TPU:0, one launch (start us, length us, event | category | flops | bytes accessed | tf_op | source)
XLA Modules:
  0.0 11.5 jit_solution(16815935338172947726)
XLA Ops:
  0.0 10.8 %normal_product.1 = f32[3,4,1024]{2,1,0:T(4,128)S(1)} custom-call(f32[3,4,1,1024]{3,2,1,0:T(1,128)} %alm_hbm.1, bf16[2,1,32,4096]{3,2,1,0:T(8,128)(2,1)} %bitcast.7, f32[2,64,4,128]{3,2,1,0:T(4,128)} %bitcast.8, f32[4,4096]{1,0:T(4,128)} %beam_hbm.1, f32[4,3]{1,0:T(4,128)} %mix_hbm.1, s32[4]{0:T(128)} %chan_hbm.1, s32[8]{0:T(128)} %order_hbm.1, ...), custom_call_target="tpu_custom_call" | custom-call | tf_op jit(solution)/shard_map/normal_product/pallas_call | solution.py:413
  10.8 0.7 %copy.10 = f32[3,4,1,1024]{3,2,1,0:T(1,128)} copy(f32[3,4,1,1024]{3,1,0,2:T(4,128)S(1)} %bitcast.6) | data formatting | bytes 98304 | tf_op jit(solution)/shard_map/reshape | solution.py:449

commit v4 on v3

--- a/solution.py
+++ b/solution.py
@@ -81,7 +81,7 @@
 
     def peer(offset):
         index = offset - 1 + (me < offset).astype(jnp.int32)
-        return lax.rem(index, chans), index // chans
+        return rest(index, chans), share(index, chans)
 
     def each(first_offset, last_offset, act):
         if last_offset - first_offset <= 64:
@@ -120,9 +120,8 @@
     for kind in range(2):
         load(leg_hbm.at[kind, 0, :, pl.ds(first, shard)], leg_v.at[kind], 2)
     for comp in range(comps):
-        for part in range(4):
-            for half in range(2):
-                load(alm_hbm.at[comp, part], comp_v.at[comp, pl.ds(4 * half + part, 1), :], 0)
+        for half in range(2):
+            load(alm_hbm.at[comp, :, 0, :], comp_v.at[comp, pl.ds(4 * half, 4), :], 0)
     load(beam_hbm.at[:, pl.ds(first, shard)], beam_v, 1)
     for stokes in range(2):
         for slot in range(slots):
@@ -135,7 +134,7 @@
         1,
         total,
         lambda offset: tell(
-            barrier, lax.rem(me_c + offset // blks, chans), lax.rem(me_b + offset % blks, blks)
+            barrier, rest(me_c + offset // blks, chans), rest(me_b + offset % blks, blks)
         ),
     )
     for copy in scalars:
@@ -160,7 +159,7 @@
     fine = orders * (2 * lane + 1).astype(F32)
     leap = orders * (2.0 * LANES)
     chunk = rest(lane, chunks).astype(F32)
-    for slot in range(slots):
+    def table(slot):
         pixels = jnp.full(grid, own_pixels[slot], F32)
         reciprocal = 1.0 / pixels
         stride = leap - jnp.floor(leap * (0.5 * reciprocal)) * (2.0 * pixels)
@@ -173,9 +172,14 @@
             ).astype(BF16)
             coarse_v[slot, block, :] = jnp.concatenate(pair_turns(*coarse_turn, order), axis=0)
 
+    for slot in range(3):
+        table(slot)
     loaded(comp_v, 0)
     loaded(beam_v, 1)
     loaded(leg_v, 2)
+    for slot in range(3, slots):
+        table(slot)
+
     low_half = iota((8, 1), 0) < 4
     keep = (iota((1, shard), 1) + first >= order_s[me_b]).astype(F32)
     alm_rows = []

time: 11.6 us -> 11.6 us (level)
  no operation moved by 1% of the time
where the time goes in v4:
time: 11.6 us; the launch traced here: 11.4 us
  Pallas kernels  10.7 us (92%)
  local copies, waits for them, and re-layouts  0.67 us (6%)
    pallas_call x1, Pallas kernels, body(): pl.pallas_call(functools.partial(kernel, chans, blks), out_shape=pltpu.VM...  10.7 us
    reshape x1, local copies, waits for them, and re-layouts, body(): return result.reshape(comp_alms.shape)  0.67 us

profile of v4, /device:TPU:0, one launch (start us, length us, event | category | flops | bytes accessed | tf_op | source)
XLA Modules:
  0.0 11.4 jit_solution(12226651967694627895)
XLA Ops:
  0.0 10.7 %normal_product.1 = f32[3,4,1024]{2,1,0:T(4,128)S(1)} custom-call(f32[3,4,1,1024]{3,2,1,0:T(1,128)} %alm_hbm.1, bf16[2,1,32,4096]{3,2,1,0:T(8,128)(2,1)} %bitcast.7, f32[2,64,4,128]{3,2,1,0:T(4,128)} %bitcast.8, f32[4,4096]{1,0:T(4,128)} %beam_hbm.1, f32[4,3]{1,0:T(4,128)} %mix_hbm.1, s32[4]{0:T(128)} %chan_hbm.1, s32[8]{0:T(128)} %order_hbm.1, ...), custom_call_target="tpu_custom_call" | custom-call | tf_op jit(solution)/shard_map/normal_product/pallas_call | solution.py:417
  10.8 0.7 %copy.10 = f32[3,4,1,1024]{3,2,1,0:T(1,128)} copy(f32[3,4,1,1024]{3,1,0,2:T(4,128)S(1)} %bitcast.6) | data formatting | bytes 98304 | tf_op jit(solution)/shard_map/reshape | solution.py:453

commit v5 on v4

--- a/solution.py
+++ b/solution.py
@@ -164,6 +164,10 @@
         reciprocal = 1.0 / pixels
         stride = leap - jnp.floor(leap * (0.5 * reciprocal)) * (2.0 * pixels)
         fine_turn = turn(fine, pixels, 2.0 * reciprocal)
+        short = pixels <= float(LANES)
+        fine_turn = [
+            jnp.where(short, value.astype(BF16).astype(F32), value) for value in fine_turn
+        ]
         coarse_turn = turn(stride * chunk, pixels, 2.0 * reciprocal)
         for order in range(blks):
             block = pl.ds(order * 4 * blks, 4 * blks)
@@ -258,21 +262,22 @@
             add_imag = outer_turn[0] * held[1] + outer_turn[1] * held[0]
             sub_real = outer_turn[2] * held[2] - outer_turn[3] * held[3]
             sub_imag = outer_turn[2] * held[3] + outer_turn[3] * held[2]
-            parts[order].append(
-                jnp.concatenate(
-                    [
-                        sub_real + add_real,
-                        sub_imag - add_imag,
-                        -sub_imag - add_imag,
-                        sub_real - add_real,
-                    ],
-                    axis=0,
-                ).astype(BF16)
+            blocks = jnp.concatenate(
+                [
+                    sub_real + add_real,
+                    sub_imag - add_imag,
+                    -sub_imag - add_imag,
+                    sub_real - add_real,
+                ],
+                axis=0,
             )
+            high = blocks.astype(BF16)
+            parts[order].append((high, (blocks - high.astype(F32)).astype(BF16)))
     ones = (share(iota((8, LANES), 1), chunks) == iota((8, LANES), 0)).astype(F32).astype(BF16)
     weight = 0.5 / by_slot(share(iota((2, lanes), 1), 4 * blks), own_pixels)
     for order in range(blks):
-        summed = dot(ones, jnp.concatenate(parts[order], axis=0), NT)
+        summed = dot(ones, jnp.concatenate([high for high, _ in parts[order]], axis=0), NT)
+        summed += dot(ones, jnp.concatenate([low for _, low in parts[order]], axis=0), NT)
         send2[order] = summed[0:2] * weight
     each(1, early + 1, lambda offset: post(offset, 1))
     each(early + 1, total, lambda offset: (post(offset, 0), post(offset, 1)))

time: 11.6 us -> 11.7 us (level)
  Pallas kernels: 10.7 us -> 10.9 us
    pallas_call x1, Pallas kernels: 10.7 us -> 10.9 us  [body(): pl.pallas_call(functools.partial(kernel, chans, blks), out_shape=pltpu.VM...]
where the time goes in v5:
time: 11.7 us; the launch traced here: 11.6 us
  Pallas kernels  10.9 us (93%)
  local copies, waits for them, and re-layouts  0.67 us (6%)
    pallas_call x1, Pallas kernels, body(): pl.pallas_call(functools.partial(kernel, chans, blks), out_shape=pltpu.VM...  10.9 us
    reshape x1, local copies, waits for them, and re-layouts, body(): return result.reshape(comp_alms.shape)  0.67 us

profile of v5, /device:TPU:0, one launch (start us, length us, event | category | flops | bytes accessed | tf_op | source)
XLA Modules:
  0.0 11.6 jit_solution(17384356162912674276)
XLA Ops:
  0.0 10.9 %normal_product.1 = f32[3,4,1024]{2,1,0:T(4,128)S(1)} custom-call(f32[3,4,1,1024]{3,2,1,0:T(1,128)} %alm_hbm.1, bf16[2,1,32,4096]{3,2,1,0:T(8,128)(2,1)} %bitcast.7, f32[2,64,4,128]{3,2,1,0:T(4,128)} %bitcast.8, f32[4,4096]{1,0:T(4,128)} %beam_hbm.1, f32[4,3]{1,0:T(4,128)} %mix_hbm.1, s32[4]{0:T(128)} %chan_hbm.1, s32[8]{0:T(128)} %order_hbm.1, ...), custom_call_target="tpu_custom_call" | custom-call | tf_op jit(solution)/shard_map/normal_product/pallas_call | solution.py:422
  10.9 0.7 %copy.10 = f32[3,4,1,1024]{3,2,1,0:T(1,128)} copy(f32[3,4,1,1024]{3,1,0,2:T(4,128)S(1)} %bitcast.6) | data formatting | bytes 98304 | tf_op jit(solution)/shard_map/reshape | solution.py:458

commit v6 on v5

--- a/solution.py
+++ b/solution.py
@@ -273,11 +273,13 @@
             )
             high = blocks.astype(BF16)
             parts[order].append((high, (blocks - high.astype(F32)).astype(BF16)))
-    ones = (share(iota((8, LANES), 1), chunks) == iota((8, LANES), 0)).astype(F32).astype(BF16)
+    ones = (
+        share(rest(iota((8, 2 * LANES), 1), LANES), chunks) == iota((8, 2 * LANES), 0)
+    ).astype(F32).astype(BF16)
     weight = 0.5 / by_slot(share(iota((2, lanes), 1), 4 * blks), own_pixels)
     for order in range(blks):
-        summed = dot(ones, jnp.concatenate([high for high, _ in parts[order]], axis=0), NT)
-        summed += dot(ones, jnp.concatenate([low for _, low in parts[order]], axis=0), NT)
+        halves = [jnp.concatenate(pair, axis=1) for pair in parts[order]]
+        summed = dot(ones, jnp.concatenate(halves, axis=0), NT)
         send2[order] = summed[0:2] * weight
     each(1, early + 1, lambda offset: post(offset, 1))
     each(early + 1, total, lambda offset: (post(offset, 0), post(offset, 1)))

time: 11.7 us -> 11.6 us (level)
    pallas_call x1, Pallas kernels: 10.9 us -> 10.8 us  [body(): pl.pallas_call(functools.partial(kernel, chans, blks), out_shape=pltpu.VM...]
where the time goes in v6:
time: 11.6 us; the launch traced here: 11.4 us
  Pallas kernels  10.8 us (93%)
  local copies, waits for them, and re-layouts  0.67 us (6%)
    pallas_call x1, Pallas kernels, body(): pl.pallas_call(functools.partial(kernel, chans, blks), out_shape=pltpu.VM...  10.8 us
    reshape x1, local copies, waits for them, and re-layouts, body(): return result.reshape(comp_alms.shape)  0.67 us

profile of v6, /device:TPU:0, one launch (start us, length us, event | category | flops | bytes accessed | tf_op | source)
XLA Modules:
  0.0 11.4 jit_solution(1134465263638182248)
XLA Ops:
  0.0 10.8 %normal_product.1 = f32[3,4,1024]{2,1,0:T(4,128)S(1)} custom-call(f32[3,4,1,1024]{3,2,1,0:T(1,128)} %alm_hbm.1, bf16[2,1,32,4096]{3,2,1,0:T(8,128)(2,1)} %bitcast.7, f32[2,64,4,128]{3,2,1,0:T(4,128)} %bitcast.8, f32[4,4096]{1,0:T(4,128)} %beam_hbm.1, f32[4,3]{1,0:T(4,128)} %mix_hbm.1, s32[4]{0:T(128)} %chan_hbm.1, s32[8]{0:T(128)} %order_hbm.1, ...), custom_call_target="tpu_custom_call" | custom-call | tf_op jit(solution)/shard_map/normal_product/pallas_call | solution.py:424
  10.8 0.7 %copy.10 = f32[3,4,1,1024]{3,2,1,0:T(1,128)} copy(f32[3,4,1,1024]{3,1,0,2:T(4,128)S(1)} %bitcast.6) | data formatting | bytes 98304 | tf_op jit(solution)/shard_map/reshape | solution.py:460

commit v7 on v6

--- a/solution.py
+++ b/solution.py
@@ -176,14 +176,11 @@
             ).astype(BF16)
             coarse_v[slot, block, :] = jnp.concatenate(pair_turns(*coarse_turn, order), axis=0)
 
-    for slot in range(3):
+    for slot in range(slots):
         table(slot)
     loaded(comp_v, 0)
     loaded(beam_v, 1)
     loaded(leg_v, 2)
-    for slot in range(3, slots):
-        table(slot)
-
     low_half = iota((8, 1), 0) < 4
     keep = (iota((1, shard), 1) + first >= order_s[me_b]).astype(F32)
     alm_rows = []

time: 11.6 us -> 11.6 us (level)
  no operation moved by 1% of the time
where the time goes in v7:
time: 11.6 us; the launch traced here: 11.4 us
  Pallas kernels  10.7 us (92%)
  local copies, waits for them, and re-layouts  0.67 us (6%)
    pallas_call x1, Pallas kernels, body(): pl.pallas_call(functools.partial(kernel, chans, blks), out_shape=pltpu.VM...  10.7 us
    reshape x1, local copies, waits for them, and re-layouts, body(): return result.reshape(comp_alms.shape)  0.67 us

profile of v7, /device:TPU:0, one launch (start us, length us, event | category | flops | bytes accessed | tf_op | source)
XLA Modules:
  0.0 11.4 jit_solution(2549221360223582318)
XLA Ops:
  0.0 10.7 %normal_product.1 = f32[3,4,1024]{2,1,0:T(4,128)S(1)} custom-call(f32[3,4,1,1024]{3,2,1,0:T(1,128)} %alm_hbm.1, bf16[2,1,32,4096]{3,2,1,0:T(8,128)(2,1)} %bitcast.7, f32[2,64,4,128]{3,2,1,0:T(4,128)} %bitcast.8, f32[4,4096]{1,0:T(4,128)} %beam_hbm.1, f32[4,3]{1,0:T(4,128)} %mix_hbm.1, s32[4]{0:T(128)} %chan_hbm.1, s32[8]{0:T(128)} %order_hbm.1, ...), custom_call_target="tpu_custom_call" | custom-call | tf_op jit(solution)/shard_map/normal_product/pallas_call | solution.py:421
  10.8 0.7 %copy.10 = f32[3,4,1,1024]{3,2,1,0:T(1,128)} copy(f32[3,4,1,1024]{3,1,0,2:T(4,128)S(1)} %bitcast.6) | data formatting | bytes 98304 | tf_op jit(solution)/shard_map/reshape | solution.py:457

commit v8 on v7

--- a/solution.py
+++ b/solution.py
@@ -238,7 +238,7 @@
             device_id_type=pl.DeviceIdType.MESH,
         ).start()
 
-    early = min(4, total - 1)
+    early = min(3, total - 1)
     pl.semaphore_wait(barrier, total - 1)
     each(1, early + 1, lambda offset: post(offset, 0))
     loaded(inv_v, 3)

time: 11.6 us -> 11.6 us (level)
  no operation moved by 1% of the time
where the time goes in v8:
time: 11.6 us; the launch traced here: 11.4 us
  Pallas kernels  10.7 us (92%)
  local copies, waits for them, and re-layouts  0.67 us (6%)
    pallas_call x1, Pallas kernels, body(): pl.pallas_call(functools.partial(kernel, chans, blks), out_shape=pltpu.VM...  10.7 us
    reshape x1, local copies, waits for them, and re-layouts, body(): return result.reshape(comp_alms.shape)  0.67 us

profile of v8, /device:TPU:0, one launch (start us, length us, event | category | flops | bytes accessed | tf_op | source)
XLA Modules:
  0.0 11.4 jit_solution(920627974635076500)
XLA Ops:
  0.0 10.7 %normal_product.1 = f32[3,4,1024]{2,1,0:T(4,128)S(1)} custom-call(f32[3,4,1,1024]{3,2,1,0:T(1,128)} %alm_hbm.1, bf16[2,1,32,4096]{3,2,1,0:T(8,128)(2,1)} %bitcast.7, f32[2,64,4,128]{3,2,1,0:T(4,128)} %bitcast.8, f32[4,4096]{1,0:T(4,128)} %beam_hbm.1, f32[4,3]{1,0:T(4,128)} %mix_hbm.1, s32[4]{0:T(128)} %chan_hbm.1, s32[8]{0:T(128)} %order_hbm.1, ...), custom_call_target="tpu_custom_call" | custom-call | tf_op jit(solution)/shard_map/normal_product/pallas_call | solution.py:421
  10.8 0.7 %copy.10 = f32[3,4,1,1024]{3,2,1,0:T(1,128)} copy(f32[3,4,1,1024]{3,1,0,2:T(4,128)S(1)} %bitcast.6) | data formatting | bytes 98304 | tf_op jit(solution)/shard_map/reshape | solution.py:457
